TPU v7x, 256 devices: a whole 4x4x8 slice. The times are simulated.
256 devices in a mesh: tok: 16 (over y, x), col: 16 (over z, core).
Axes of the slice: x: 4, y: 4, z: 8, core: 2. Of those that a mesh axis runs over, the one named last changes fastest.
Arguments:
- activations: bfloat16 [32768, 8192], P('tok', 'col'), may hold values from -60 to 60, as said below
- weight: bfloat16 [8192, 8192], P('tok', 'col'), may hold values from -6 to 6
- keep_mask: int32 [8192, 8192], P('tok', 'col'), may hold values from 0 to 1
Outputs:
- new_weight: bfloat16 [8192, 8192], P('tok', 'col')
Inputs may be any that keep to these rules, and one draw needn't show every extreme that they name: activations of calibration tokens.
All inputs are finite; a program needn't handle non-finite values.
Results may differ from a plain program's by a relative error of at most 0.00115.
Values may be sent and summed in bfloat16 or wider, within the bound.
A program may use at most 64 MiB of HBM per device.

v0:
```python
import jax
import jax.numpy as jnp
from jax import lax
from jax.sharding import PartitionSpec as P

B = 1024
ITERS = 4


def per_device(activations, weight, keep_mask):
    highest = lax.Precision.HIGHEST
    n_col = lax.axis_size("col")
    n_tok = lax.axis_size("tok")
    tok_rows = activations.shape[0]
    panel_width = B // n_col
    total_count = tok_rows * n_tok
    partial_panel = lax.dot_general(
        activations,
        lax.all_gather(activations[:, :panel_width], "col", axis=1, tiled=True),
        (((0,), (0,)), ((), ())),
        preferred_element_type=jnp.float32,
    )
    hessian_panel = lax.psum(partial_panel, "tok") / total_count
    block_part = hessian_panel[:panel_width]
    diagonal_block = lax.all_gather(block_part, "col", axis=0, tiled=True)
    identity = jnp.eye(B, dtype=jnp.float32)
    damping = 0.01 * jnp.mean(jnp.diagonal(diagonal_block))
    damped = diagonal_block + damping * identity
    frobenius = jnp.sqrt(jnp.sum(damped * damped))
    col_index = lax.axis_index("col")
    row_ids = col_index * panel_width + lax.iota(jnp.int32, panel_width)
    iterate = (row_ids[:, None] == lax.iota(jnp.int32, B)[None, :]).astype(jnp.float32) / frobenius
    for sweep in range(ITERS):
        if sweep == 0:
            whole = identity / frobenius
        else:
            whole = lax.all_gather(iterate.astype(jnp.bfloat16), "col", axis=0, tiled=True).astype(
                iterate.dtype
            )
        product = jnp.dot(iterate, damped, precision=highest)
        iterate = 2.0 * iterate - jnp.dot(product, whole, precision=highest)
    inverse = lax.all_gather(iterate, "col", axis=0, tiled=True)
    pruned = jnp.where(
        keep_mask[:, :panel_width] == 0, weight[:, :panel_width], jnp.zeros((), jnp.bfloat16)
    )
    pruned_panel = lax.all_gather(pruned, "col", axis=1, tiled=True).astype(jnp.float32)
    factor_rows = jnp.dot(pruned_panel, inverse, precision=highest)
    correction = lax.dot_general(
        factor_rows, hessian_panel, (((1,), (1,)), ((), ())), precision=highest
    )
    kept = keep_mask.astype(jnp.float32)
    return (kept * (weight.astype(jnp.float32) - correction)).astype(jnp.bfloat16)


def solution(mesh):
    return jax.shard_map(
        per_device,
        mesh=mesh,
        in_specs=(P("tok", "col"), P("tok", "col"), P("tok", "col")),
        out_specs=P("tok", "col"),
        check_vma=False,
    )
```

profile of v0, /device:TPU:1, one launch (start us, length us, event | category | flops | bytes accessed | tf_op | source)
XLA Modules:
  0.0 456.3 jit_solution(11155648659330884020)
XLA Ops:
  6.5 1.1 slice.14
  7.6 0.9 copy.9
  8.6 47.0 %all-gather.10.cloned.1.call-done = bf16[2048,1024]{0,1:T(8,128)(2,1)} async-done(((bf16[2048,64]{0,1:T(8,128)(2,1)}), bf16[2048,1024]{0,1:T(8,128)(2,1)}) %all-gather.10.cloned.1.call-update) | async-done | bytes 4194320 | tf_op jit(solution)/shard_map/all_gather | solution.py:19
  55.5 6.6 %fusion.25 = f32[512,1024]{1,0:T(8,128)} fusion(bf16[2048,512]{1,0:T(8,128)(2,1)} %param.3, bf16[2048,1024]{0,1:T(8,128)(2,1)} %all-gather.10.cloned.1.call-done), kind=kOutput, calls=%fused_computation.37 | convolution fusion | flops 2147483648 | bytes 8388608 | tf_op jit(solution)/shard_map/dot_general | solution.py:17
  62.2 97.5 %all-reduce.2.cloned.1.call-done = f32[512,1024]{1,0:T(8,128)} async-done(((f32[512,1024]{1,0:T(8,128)}), f32[512,1024]{1,0:T(8,128)}) %all-reduce.2.cloned.1.call-update) | async-done | bytes 2097168 | tf_op jit(solution)/shard_map/psum | solution.py:23
  159.7 1.8 broadcast_multiply_fusion
  162.3 43.1 %all-gather.12.cloned.1.call-done = f32[1024,1024]{1,0:T(8,128)} async-done(((f32[64,1024]{1,0:T(8,128)}), f32[1024,1024]{1,0:T(8,128)}) %all-gather.12.cloned.1.call-update) | async-done | bytes 4194320 | tf_op jit(solution)/shard_map/all_gather | solution.py:25
  205.5 17.2 %gather_fusion = f32[1024]{0:T(1024)S(1)} fusion(f32[1024,1024]{1,0:T(8,128)} %all-gather.12.cloned.1.call-done, s32[1024]{0:T(1024)S(1)} %bitcast.16), kind=kCustom, calls=%fused_computation | custom fusion | bytes 16384 | tf_op jit(solution)/shard_map/jit(diagonal)/cond/branch_0_fun/gather | solution.py:27
  223.9 3.9 multiply_reduce_fusion
  228.5 4.9 %fusion.9 = f32[64,1024]{1,0:T(8,128)S(1)} fusion(f32[1024,1024]{1,0:T(8,128)} %all-gather.12.cloned.1.call-done, f32[]{:T(128)S(6)} %mul_shard_map.3, f32[]{:T(128)S(6)} %sqrt.3, s32[64]{0:T(128)S(1)} %iota_add_fusion), kind=kOutput, calls=%fused_computation.14 | convolution fusion | flops 808583168 | bytes 4456712 | tf_op jit(solution)/shard_map/dot_general | solution.py:40
  233.4 1.9 fusion.22
  235.4 4.9 %fusion.8 = f32[64,1024]{1,0:T(8,128)S(1)} fusion(f32[64,1024]{1,0:T(8,128)S(1)} %get-tuple-element.6, f32[1024,1024]{1,0:T(8,128)} %all-gather.12.cloned.1.call-done, f32[]{:T(128)S(6)} %mul_shard_map.3), kind=kOutput, calls=%fused_computation.13 | convolution fusion | flops 808452096 | bytes 4718596 | tf_op jit(solution)/shard_map/dot_general | solution.py:40
  240.3 33.5 %all-gather.14.cloned.1.call-done = bf16[1024,1024]{1,0:T(8,128)(2,1)} async-done(((bf16[64,1024]{1,0:T(8,128)(2,1)}), bf16[1024,1024]{1,0:T(8,128)(2,1)}) %all-gather.14.cloned.1.call-update) | async-done | bytes 2097168 | tf_op jit(solution)/shard_map/all_gather | solution.py:37
  273.8 3.5 fusion.23
  277.5 4.9 %fusion.7 = f32[64,1024]{1,0:T(8,128)S(1)} fusion(f32[64,1024]{1,0:T(8,128)S(1)} %get-tuple-element.8, f32[1024,1024]{1,0:T(8,128)} %all-gather.12.cloned.1.call-done, f32[]{:T(128)S(6)} %mul_shard_map.3), kind=kOutput, calls=%fused_computation.12 | convolution fusion | flops 808452096 | bytes 4718596 | tf_op jit(solution)/shard_map/dot_general | solution.py:40
  282.5 33.0 %all-gather.16.cloned.1.call-done = bf16[1024,1024]{1,0:T(8,128)(2,1)} async-done(((bf16[64,1024]{1,0:T(8,128)(2,1)}), bf16[1024,1024]{1,0:T(8,128)(2,1)}) %all-gather.16.cloned.1.call-update) | async-done | bytes 2097168 | tf_op jit(solution)/shard_map/all_gather | solution.py:37
  315.5 3.5 fusion.24
  320.0 4.9 %fusion.6 = f32[64,1024]{1,0:T(8,128)S(1)} fusion(f32[64,1024]{1,0:T(8,128)S(1)} %get-tuple-element.10, f32[1024,1024]{1,0:T(8,128)} %all-gather.12.cloned.1.call-done, f32[]{:T(128)S(6)} %mul_shard_map.3), kind=kOutput, calls=%fused_computation.11 | convolution fusion | flops 808452096 | bytes 4718596 | tf_op jit(solution)/shard_map/dot_general | solution.py:40
  324.9 32.3 %all-gather.18.cloned.1.call-done = bf16[1024,1024]{1,0:T(8,128)(2,1)} async-done(((bf16[64,1024]{1,0:T(8,128)(2,1)}), bf16[1024,1024]{1,0:T(8,128)(2,1)}) %all-gather.18.cloned.1.call-update) | async-done | bytes 2097168 | tf_op jit(solution)/shard_map/all_gather | solution.py:37
  357.2 3.5 convolution_subtract_fusion.1
  360.7 35.4 %all-gather.8.cloned.1.call-done = bf16[512,1024]{0,1:T(8,128)(2,1)} async-done(((bf16[512,64]{0,1:T(8,128)(2,1)}), bf16[512,1024]{0,1:T(8,128)(2,1)}) %all-gather.8.cloned.1.call-update) | async-done | bytes 1048592 | tf_op jit(solution)/shard_map/all_gather | solution.py:46
  396.1 42.8 %all-gather.20.cloned.1.call-done = f32[1024,1024]{1,0:T(8,128)} async-done(((f32[64,1024]{1,0:T(8,128)}), f32[1024,1024]{1,0:T(8,128)}) %all-gather.20.cloned.1.call-update) | async-done | bytes 4194320 | tf_op jit(solution)/shard_map/all_gather | solution.py:42
  438.9 6.1 %fusion.26 = f32[512,1024]{1,0:T(8,128)S(1)} fusion(bf16[512,1024]{0,1:T(8,128)(2,1)} %all-gather.8.cloned.1.call-done, f32[1024,1024]{1,0:T(8,128)} %all-gather.20.cloned.1.call-done), kind=kOutput, calls=%fused_computation.38 | convolution fusion | flops 6442450944 | bytes 7340032 | tf_op jit(solution)/shard_map/dot_general | solution.py:47
  445.0 4.5 fusion.5
  (33 shorter events, 2.8 us)
Async XLA Ops:
  6.5 49.0 %all-gather.10.cloned.1.call-start = ((), (), s32[]{:S(2)}) async-start(), calls=%async_computation.1 | async-start | bytes 4456448 | tf_op jit(solution)/shard_map/all_gather | solution.py:19
  8.5 151.2 %all-reduce.2.cloned.1.call-start = ((), (), s32[]{:S(2)}) async-start(), calls=%async_computation.2 | async-start | bytes 4194304 | tf_op jit(solution)/shard_map/psum | solution.py:23
  62.2 143.3 %all-gather.12.cloned.1.call-start = ((), (), s32[]{:S(2)}) async-start(), calls=%async_computation.3 | async-start | bytes 4456448 | tf_op jit(solution)/shard_map/all_gather | solution.py:25
  162.3 111.5 %all-gather.14.cloned.1.call-start = ((), (), s32[]{:S(2)}) async-start(), calls=%async_computation.4 | async-start | bytes 2228224 | tf_op jit(solution)/shard_map/all_gather | solution.py:37
  235.3 80.1 %all-gather.16.cloned.1.call-start = ((), (), s32[]{:S(2)}) async-start(), calls=%async_computation.5 | async-start | bytes 2228224 | tf_op jit(solution)/shard_map/all_gather | solution.py:37
  277.3 79.9 %all-gather.18.cloned.1.call-start = ((), (), s32[]{:S(2)}) async-start(), calls=%async_computation.6 | async-start | bytes 2228224 | tf_op jit(solution)/shard_map/all_gather | solution.py:37
  277.5 41.5 %slice-start = ((s32[512,512]{1,0:T(8,128)}), s32[512,64]{1,0:T(8,128)S(1)}, s32[]{:S(2)}) async-start(s32[512,512]{1,0:T(8,128)} %param.5), calls=%async_computation.8 | async-start | bytes 524288 | tf_op jit(solution)/shard_map/slice | solution.py:44
  277.5 41.6 %slice-start.1 = ((bf16[512,512]{1,0:T(8,128)(2,1)}), bf16[512,64]{1,0:T(8,128)(2,1)S(1)}, s32[]{:S(2)}) async-start(bf16[512,512]{1,0:T(8,128)(2,1)} %param.4), calls=%async_computation.9 | async-start | bytes 262144 | tf_op jit(solution)/shard_map/slice | solution.py:44
  319.0 77.2 %all-gather.8.cloned.1.call-start = ((), (), s32[]{:S(2)}) async-start(), calls=%async_computation | async-start | bytes 1114112 | tf_op jit(solution)/shard_map/all_gather | solution.py:46
  319.9 119.0 %all-gather.20.cloned.1.call-start = ((), (), s32[]{:S(2)}) async-start(), calls=%async_computation.7 | async-start | bytes 4456448 | tf_op jit(solution)/shard_map/all_gather | solution.py:42
  360.7 84.3 %copy-start = (f32[512,1024]{1,0:T(8,128)S(1)}, f32[512,1024]{1,0:T(8,128)}, u32[]{:S(2)}) copy-start(f32[512,1024]{1,0:T(8,128)} %all-reduce.2.cloned.1.call-done) | copy-start | bytes 6291460
  360.7 84.3 %copy-start.1 = (s32[512,512]{1,0:T(8,128)S(1)}, s32[512,512]{1,0:T(8,128)}, u32[]{:S(2)}) copy-start(s32[512,512]{1,0:T(8,128)} %param.5) | copy-start | bytes 3145732
  438.9 6.1 %copy-start.2 = (bf16[512,512]{1,0:T(8,128)(2,1)S(1)}, bf16[512,512]{1,0:T(8,128)(2,1)}, u32[]{:S(2)}) copy-start(bf16[512,512]{1,0:T(8,128)(2,1)} %param.4) | copy-start | bytes 1572868
Sparse Core Ops, SparseCore 0:
  9.2 46.3 all-gather.9
  62.3 97.4 all-reduce.1
  162.4 43.0 all-gather.11
  235.5 38.2 all-gather.13
  277.4 38.0 all-gather.15
  319.1 38.0 all-gather.17
  359.1 36.9 all-gather.7
  398.1 40.7 all-gather.19
where the time goes:
time: 457 us; the launch traced here: 456 us
  waiting for transfers between devices  365 us (80%)
  matrix products  49.1 us (11%)
  local copies, waits for them, and re-layouts  20.1 us (4%)
  between operations  15 us (3%)
  other arithmetic  6.89 us (2%)
    all_gather x3, waiting for transfers between devices, per_device(): lax.all_gather(iterate.astype(jnp.bfloat16), 'col', axis=0, tiled=True)  98.8 us
    psum x1, waiting for transfers between devices, per_device(): hessian_panel = lax.psum(partial_panel, 'tok') / total_count  97.5 us
    all_gather x1, waiting for transfers between devices, per_device(): lax.all_gather(activations[:, :panel_width], 'col', axis=1, tiled=True)  47 us
    all_gather x1, waiting for transfers between devices, per_device(): diagonal_block = lax.all_gather(block_part, 'col', axis=0, tiled=True)  43.1 us
    all_gather x1, waiting for transfers between devices, per_device(): inverse = lax.all_gather(iterate, 'col', axis=0, tiled=True)  42.8 us
    all_gather x1, waiting for transfers between devices, per_device(): lax.all_gather(pruned, 'col', axis=1, tiled=True).astype(jnp.float32)  35.4 us
    dot_general x4, matrix products, per_device(): product = jnp.dot(iterate, damped, precision=highest)  19.6 us
    gather x1, local copies, waits for them, and re-layouts, per_device(): damping = 0.01 * jnp.mean(jnp.diagonal(diagonal_block))  17.2 us
  transfers between devices with their start and end apart: 8, of which 8 were waited for; matrix products, arithmetic and copies ran while one was open for 4% of the time, Pallas kernels for 0%

commit v1 on v0

v1 whole, which is shorter than its diff:
```python
import jax
import jax.numpy as jnp
from jax import lax
from jax.sharding import PartitionSpec as P

B = 1024
ITERS = 4


def split(x):
    high = lax.reduce_precision(x, exponent_bits=8, mantissa_bits=7)
    return high.astype(jnp.bfloat16), (x - high).astype(jnp.bfloat16)


def mm(a, b, dims=(((1,), (0,)), ((), ()))):
    return lax.dot_general(a, b, dims, preferred_element_type=jnp.float32)


def per_device(activations, weight, keep_mask):
    n_col = lax.axis_size("col")
    n_tok = lax.axis_size("tok")
    tok_rows = activations.shape[0]
    panel_width = B // n_col
    total_count = tok_rows * n_tok
    pruned = jnp.where(
        keep_mask[:, :panel_width] == 0, weight[:, :panel_width], jnp.zeros((), jnp.bfloat16)
    )
    panel = lax.all_gather(activations[:, :panel_width], "col", axis=1, tiled=True)
    partial_panel = mm(activations, panel, (((0,), (0,)), ((), ())))
    pruned_panel = lax.all_gather(pruned, "col", axis=1, tiled=True)
    hessian_panel = lax.psum(partial_panel, "tok") / total_count
    block = lax.all_gather(hessian_panel[:panel_width], "col", axis=0, tiled=True)
    rows = lax.broadcasted_iota(jnp.int32, (B, B), 0)
    columns = lax.broadcasted_iota(jnp.int32, (B, B), 1)
    on_diagonal = rows == columns
    mean_diagonal = jnp.sum(jnp.where(on_diagonal, block, 0.0)) / B
    damped = block + jnp.where(on_diagonal, 0.01 * mean_diagonal, 0.0)
    scale = lax.rsqrt(jnp.sum(damped * damped))
    g = damped * scale
    y = pruned_panel.astype(jnp.float32)
    for sweep in range(ITERS):
        g_high = g.astype(jnp.bfloat16)
        y_high, y_low = split(y)
        y = 2.0 * y - (mm(y_high, g_high) + mm(y_low, g_high))
        if sweep < ITERS - 1:
            g = 2.0 * g - mm(g_high, g_high)
    y_high, y_low = split(y * scale)
    h_high, h_low = split(hessian_panel)
    nt = (((1,), (1,)), ((), ()))
    correction = mm(y_high, h_high, nt) + mm(y_low, h_high, nt) + mm(y_high, h_low, nt)
    kept = keep_mask.astype(jnp.float32)
    return (kept * (weight.astype(jnp.float32) - correction)).astype(jnp.bfloat16)


def solution(mesh):
    return jax.shard_map(
        per_device,
        mesh=mesh,
        in_specs=(P("tok", "col"), P("tok", "col"), P("tok", "col")),
        out_specs=P("tok", "col"),
        check_vma=False,
    )
```

time: 457 us -> 285 us (0.62)
  waiting for transfers between devices: 365 us -> 223 us
  matrix products: 49.1 us -> 31.6 us
  local copies, waits for them, and re-layouts: 20.1 us -> 6.38 us
    all_gather x6 -> x2, waiting for transfers between devices: 220 us -> 80 us  [the longest x1 41 us: per_device(): lax.all_gather(hessian_panel[:panel_width], 'col', axis=0, tiled=True)]
    dot_general x11 -> x15, matrix products: 49.1 us -> 31.6 us  [mm(): return lax.dot_general(a, b, dims, preferred_element_type=jnp.float32)]
    gather x1 -> x0, local copies, waits for them, and re-layouts: 17.2 us -> none  [per_device(): damping = 0.01 * jnp.mean(jnp.diagonal(diagonal_block))]
  transfers between devices with their start and end apart: 8 -> 4, of which waited for: 8 -> 4; matrix products, arithmetic and copies ran while one was open for 4% -> 2% of each run, Pallas kernels for 0% -> 0%
where the time goes in v1:
time: 285 us
  waiting for transfers between devices  223 us (78%)
  matrix products  31.6 us (11%)
  between operations  14.6 us (5%)
  other arithmetic  9.21 us (3%)
  local copies, waits for them, and re-layouts  6.38 us (2%)
    psum x1, waiting for transfers between devices, per_device(): hessian_panel = lax.psum(partial_panel, 'tok') / total_count  95.8 us
    all_gather x1, waiting for transfers between devices, per_device(): lax.all_gather(activations[:, :panel_width], 'col', axis=1, tiled=True)  46.8 us
    all_gather x1, waiting for transfers between devices, per_device(): lax.all_gather(hessian_panel[:panel_width], 'col', axis=0, tiled=True)  41 us
    all_gather x1, waiting for transfers between devices, per_device(): pruned_panel = lax.all_gather(pruned, 'col', axis=1, tiled=True)  39 us
    dot_general x15, matrix products, mm(): return lax.dot_general(a, b, dims, preferred_element_type=jnp.float32)  31.6 us
  transfers between devices with their start and end apart: 4, of which 4 were waited for; matrix products, arithmetic and copies ran while one was open for 2% of the time, Pallas kernels for 0%

profile of v1, /device:TPU:1, one launch (start us, length us, event | category | flops | bytes accessed | tf_op | source)
XLA Modules:
  0.0 284.6 jit_solution(3406045359667828655)
XLA Ops:
  6.5 1.2 slice.14
  7.8 0.9 copy.10
  8.7 46.8 %all-gather.6.cloned.1.call-done = bf16[2048,1024]{0,1:T(8,128)(2,1)} async-done(((bf16[2048,64]{0,1:T(8,128)(2,1)}), bf16[2048,1024]{0,1:T(8,128)(2,1)}) %all-gather.6.cloned.1.call-update) | async-done | bytes 4194320 | tf_op jit(solution)/shard_map/all_gather | solution.py:28
  55.6 5.9 %fusion.29 = f32[512,1024]{1,0:T(8,128)} fusion(bf16[2048,512]{1,0:T(8,128)(2,1)S(1)} %copy-done.4, bf16[2048,1024]{0,1:T(8,128)(2,1)} %all-gather.6.cloned.1.call-done), kind=kOutput, calls=%fused_computation.50 | convolution fusion | flops 2147483648 | bytes 8388608 | tf_op jit(solution)/shard_map/dot_general | solution.py:16
  61.5 0.8 slice-done.1
  63.3 95.8 %all-reduce.2.cloned.1.call-done = f32[512,1024]{1,0:T(8,128)} async-done(((f32[512,1024]{1,0:T(8,128)}), f32[512,1024]{1,0:T(8,128)}) %all-reduce.2.cloned.1.call-update) | async-done | bytes 2097168 | tf_op jit(solution)/shard_map/psum | solution.py:31
  159.1 1.8 broadcast_multiply_fusion
  161.6 39.0 %all-gather.4.cloned.1.call-done = bf16[512,1024]{0,1:T(8,128)(2,1)} async-done(((bf16[512,64]{0,1:T(8,128)(2,1)}), bf16[512,1024]{0,1:T(8,128)(2,1)}) %all-gather.4.cloned.1.call-update) | async-done | bytes 1048592 | tf_op jit(solution)/shard_map/all_gather | solution.py:30
  200.6 1.7 copy.6
  202.3 41.0 %all-gather.8.cloned.1.call-done = f32[1024,1024]{1,0:T(8,128)} async-done(((f32[64,1024]{1,0:T(8,128)}), f32[1024,1024]{1,0:T(8,128)}) %all-gather.8.cloned.1.call-update) | async-done | bytes 4194320 | tf_op jit(solution)/shard_map/all_gather | solution.py:32
  243.3 2.9 %select_reduce_fusion = f32[]{:T(128)} fusion(f32[1024,1024]{1,0:T(8,128)} %all-gather.8.cloned.1.call-done), kind=kLoop, calls=%fused_computation.5 | loop fusion | flops 3145727 | bytes 4194308 | tf_op jit(solution)/shard_map/reduce_sum | solution.py:36
  246.9 3.9 %multiply_reduce_fusion = f32[]{:T(128)} fusion(f32[1024,1024]{1,0:T(8,128)} %all-gather.8.cloned.1.call-done, f32[]{:T(128)S(6)} %mul_shard_map.3), kind=kLoop, calls=%fused_computation.3 | loop fusion | flops 5242879 | bytes 4194312 | tf_op jit(solution)/shard_map/reduce_sum | solution.py:38
  251.4 7.0 %multiply_subtract_fusion.1 = f32[1024,1024]{1,0:T(8,128)S(1)} fusion(f32[1024,1024]{1,0:T(8,128)} %all-gather.8.cloned.1.call-done, f32[]{:T(128)S(6)} %rsqrt.3, f32[]{:T(128)S(6)} %mul_shard_map.3), kind=kOutput, calls=%fused_computation.2 | convolution fusion | flops 2159017984 | bytes 8388616 | tf_op jit(solution)/shard_map/dot_general | solution.py:16
  258.5 2.3 multiply_subtract_fusion
  260.8 1.3 fusion.20
  262.1 1.4 fusion.6
  263.5 1.3 fusion.17
  264.8 1.3 add_subtract_fusion.1
  266.2 2.4 subtract_convert_fusion
  268.5 1.3 fusion.18
  269.8 1.6 add_subtract_fusion
  271.5 1.3 fusion.19
  272.7 1.4 subtract_multiply_fusion
  276.4 1.6 fusion.10
  (27 shorter events, 4.1 us)
Async XLA Ops:
  6.5 49.0 %copy-start.4 = (bf16[2048,512]{1,0:T(8,128)(2,1)S(1)}, bf16[2048,512]{1,0:T(8,128)(2,1)}, u32[]{:S(2)}) copy-start(bf16[2048,512]{1,0:T(8,128)(2,1)} %param.3) | copy-start | bytes 6291460
  6.5 49.0 %all-gather.6.cloned.1.call-start = ((), (), s32[]{:S(2)}) async-start(), calls=%async_computation.1 | async-start | bytes 4456448 | tf_op jit(solution)/shard_map/all_gather | solution.py:28
  8.7 150.4 %all-reduce.2.cloned.1.call-start = ((), (), s32[]{:S(2)}) async-start(), calls=%async_computation.2 | async-start | bytes 4194304 | tf_op jit(solution)/shard_map/psum | solution.py:31
  61.5 0.9 slice-start.1
  61.5 1.0 slice-start
  61.5 139.1 %all-gather.4.cloned.1.call-start = ((), (), s32[]{:S(2)}) async-start(), calls=%async_computation | async-start | bytes 1114112 | tf_op jit(solution)/shard_map/all_gather | solution.py:30
  63.3 180.0 %all-gather.8.cloned.1.call-start = ((), (), s32[]{:S(2)}) async-start(), calls=%async_computation.3 | async-start | bytes 4456448 | tf_op jit(solution)/shard_map/all_gather | solution.py:32
  258.5 2.4 copy-start.1
  272.7 1.6 copy-start
  275.1 1.2 copy-start.2
  275.1 1.3 copy-start.3
Sparse Core Ops, SparseCore 0:
  9.2 46.3 all-gather.5
  61.6 97.4 all-reduce.1
  161.1 39.5 all-gather.3
  202.4 40.7 all-gather.7

commit v2 on v1

v2 whole, which is shorter than its diff:
```python
import functools

import jax
import jax.numpy as jnp
from jax import lax
from jax.experimental import pallas as pl
from jax.experimental.pallas import tpu as pltpu
from jax.sharding import PartitionSpec as P

B = 1024
ITERS = 4
NZ, NY, NX, NT, NQ = 8, 4, 4, 16, 16
WIDTH = 64
OFFSETS = (0, -1, 1, -2, 2, -3, 3, 4)
GROUPS = ((0, 1), (1, 2), (3, 2), (5, 2), (7, 1))
BF, F32 = jnp.bfloat16, jnp.float32


def dot(a, b):
    return jnp.dot(a, b, preferred_element_type=F32)


def hop(d, k, v):
    return d * 7 + (k - 1) * 2 + (v if k < 4 else 0)


def units(d, k):
    return (0, 1) if k < 4 else (d,)


def kernel(
    a_hbm, w_hbm, m_hbm, out_ref,
    a, w, m, pt, hts, rsr, red, dsend, drecv, dzs, drho, g, gb, hta, hh, hl, pts, pall, y, yb, yx,
    load_sem, sib_s, sib_r, ring_s, ring_r, fwd_s, fwd_r, rs_s, rs_r, dsib_s, dsib_r, dz_s, dz_r,
    dxy_s, dxy_r, df_s, df_r, pz_s, pz_r, ha_s, ha_r, yx_s, yx_r,
):
    t, q = lax.axis_index("tok"), lax.axis_index("col")
    ty, tx = lax.div(t, NX), lax.rem(t, NX)
    z, c = lax.div(q, 2), lax.rem(q, 2)
    other = 1 - c
    sibling = 2 * z + other
    inverse_count = 1.0 / (a.shape[0] * NT)

    def send(src, dst, send_sem, recv_sem, tok, col):
        pltpu.make_async_remote_copy(
            src_ref=src, dst_ref=dst, send_sem=send_sem, recv_sem=recv_sem,
            device_id=(tok, col), device_id_type=pl.DeviceIdType.MESH,
        ).start()

    def wait(ref, sem):
        pltpu.make_async_copy(ref, ref, sem).wait()

    def each(first, last, body):
        def step(i, carry):
            body(i)
            return carry
        lax.fori_loop(first, last, step, 0)

    loads = [
        pltpu.make_async_copy(a_hbm.at[:, 0:128], a.at[:, 0:128], load_sem.at[0]),
        pltpu.make_async_copy(a_hbm.at[:, 128:512], a.at[:, 128:512], load_sem.at[1]),
        pltpu.make_async_copy(w_hbm, w, load_sem.at[2]),
        pltpu.make_async_copy(m_hbm, m, load_sem.at[3]),
    ]
    for load in loads:
        load.start()

    barrier = pltpu.get_barrier_semaphore()

    def greet(i):
        pl.semaphore_signal(
            barrier, inc=1, device_id=(lax.rem(t + i, NT), q), device_id_type=pl.DeviceIdType.MESH
        )
        pl.semaphore_signal(
            barrier, inc=1, device_id=(t, lax.rem(q + i, NQ)), device_id_type=pl.DeviceIdType.MESH
        )

    each(1, 16, greet)

    loads[0].wait()
    for half in range(2):
        for part in range(2):
            rows = half * 1024 + part * 512
            piece = a[rows:rows + 512, 0:128].astype(F32).T
            pt[z, half, c, :, part * 512:(part + 1) * 512] = piece[0:WIDTH].astype(BF)
    pl.semaphore_wait(barrier, 30)

    def ring(d, k, v, origin):
        u = c if v == 0 else other
        ref = pt.at[origin, c, u]
        to = lax.rem(z + (1 if d == 0 else NZ - 1), NZ)
        send(ref, ref, ring_s.at[hop(d, k, v)], ring_r.at[hop(d, k, v)], t, 2 * to + c)

    send(pt.at[z, other, c], pt.at[z, other, c], sib_s.at[0], sib_r.at[0], t, sibling)
    ring(0, 1, 0, z)
    ring(1, 1, 0, z)
    send(pt.at[z, c, c], pt.at[z, c, c], sib_s.at[1], sib_r.at[1], t, sibling)
    wait(pt.at[z, c, other], sib_r.at[0])
    ring(0, 1, 1, z)
    ring(1, 1, 1, z)

    loads[2].wait()
    loads[3].wait()
    pruned = jnp.where(m[:, 0:128] == 0, w[:, 0:128].astype(F32), 0.0).T
    pts[0] = pruned[0:WIDTH, 0:256].astype(BF)
    pts[1] = pruned[0:WIDTH, 256:512].astype(BF)
    pall[q] = pts[c]

    loads[1].wait()
    wait(pt.at[z, other, other], sib_r.at[1])

    def chunk_at(slot):
        return lax.rem(z + OFFSETS[slot] + NZ, NZ)

    def partial_panel(group):
        first, n = GROUPS[group]
        total = None
        for half in range(2):
            lhs = [pt[chunk_at(first + i), half].reshape(128, 1024) for i in range(n)]
            lhs = lhs[0] if n == 1 else jnp.concatenate(lhs, axis=0)
            term = dot(lhs, a[half * 1024:(half + 1) * 1024, :])
            total = term if total is None else total + term
        for i in range(n):
            hts[:, first + i] = total[128 * i:128 * (i + 1)].reshape(16, 8, 512)
        rsr[t, first:first + n] = hts[t, first:first + n]

        def share(i):
            to = lax.rem(t + i, NT)
            send(
                hts.at[to, first:first + n], rsr.at[t, first:first + n],
                rs_s.at[group], rs_r.at[group], to, q,
            )

        each(1, 16, share)

    def reduce_group(group):
        first, n = GROUPS[group]
        wait(rsr.at[0:15, first:first + n], rs_r.at[group])
        for i in range(n):
            total = rsr[0, first + i]
            for source in range(1, NT):
                total = total + rsr[source, first + i]
            red[chunk_at(first + i)] = total * inverse_count

    partial_panel(0)
    for k in range(1, 5):
        for v in range(2):
            for d in range(2):
                if v not in units(d, k):
                    continue
                origin = lax.rem(z + (NZ - k if d == 0 else k), NZ)
                u = c if v == 0 else other
                ref = pt.at[origin, c, u]
                wait(ref, ring_r.at[hop(d, k, v)])
                if k < 4 and v in units(d, k + 1):
                    ring(d, k + 1, v, origin)
                send(ref, ref, fwd_s.at[hop(d, k, v)], fwd_r.at[hop(d, k, v)], t, sibling)
        for v in range(2):
            for d in range(2):
                if v in units(d, k):
                    origin = lax.rem(z + (NZ - k if d == 0 else k), NZ)
                    wait(pt.at[origin, other, other if v == 0 else c], fwd_r.at[hop(d, k, v)])
        partial_panel(k)
        if k >= 2:
            reduce_group(k - 2)
    reduce_group(3)
    reduce_group(4)

    lanes = lax.broadcasted_iota(jnp.int32, (64, 128), 1)
    own = red[:, :, 0:128].reshape(64, 128)
    own = jnp.where(c == 0, own, pltpu.roll(own, 64, 1))
    own = jnp.where(lax.div(lanes, 64) == c, own, 0.0)
    dsend[0] = own[0:32].astype(BF)
    dsend[1] = own[32:64].astype(BF)
    send(dsend.at[other], drecv, dsib_s.at[0], dsib_r.at[0], t, sibling)
    hta[:, ty, tx] = red[...]
    wait(drecv, dsib_r.at[0])
    here = (dsend[c].astype(F32) + drecv[...].astype(F32)).astype(BF).reshape(2, 16, 128)
    dzs[...] = here
    my_lanes = pl.ds(pl.multiple_of(z * 128, 128), 128)
    drho[ty, tx, c, :, :, my_lanes] = here

    def along_z(i):
        send(
            dzs, drho.at[ty, tx, c, :, :, my_lanes], dz_s.at[0], dz_r.at[0],
            t, 2 * lax.rem(z + i, NZ) + c,
        )

    each(1, NZ, along_z)

    def share_pruned(i):
        to = lax.rem(q + i, NQ)
        send(pts.at[lax.rem(to, 2)], pall.at[q], pz_s.at[0], pz_r.at[0], t, to)

    each(1, NQ, share_pruned)

    wait(drho.at[ty, tx, c, :, :, 0:896], dz_r.at[0])

    def along_x(i):
        return NX * ty + lax.rem(tx + i, NX)

    def along_y(i):
        return NX * lax.rem(ty + i, NY) + tx

    for i in range(1, 4):
        ref = drho.at[ty, tx, c, 0]
        send(ref, ref, dxy_s.at[0], dxy_r.at[0], along_x(i), q)
        ref = drho.at[ty, tx, c, 1]
        send(ref, ref, dxy_s.at[1], dxy_r.at[1], along_y(i), q)
    wait(drho.at[0, 0:3, c, 0], dxy_r.at[0])
    for i in range(1, 4):
        ref = drho.at[ty, :, c, 0]
        send(ref, ref, dxy_s.at[2], dxy_r.at[2], along_y(i), q)
    wait(drho.at[0, 0:3, c, 1], dxy_r.at[1])
    for i in range(1, 4):
        ref = drho.at[:, tx, c, 1]
        send(ref, ref, dxy_s.at[3], dxy_r.at[3], along_x(i), q)
    ref = drho.at[ty, :, c, 0]
    send(ref, ref, df_s.at[0], df_r.at[0], t, sibling)
    ref = drho.at[:, tx, c, 1]
    send(ref, ref, df_s.at[1], df_r.at[1], t, sibling)

    for i in range(1, 4):
        ref = hta.at[0:4, ty, tx]
        send(ref, ref, ha_s.at[0], ha_r.at[0], along_x(i), q)
        ref = hta.at[4:8, ty, tx]
        send(ref, ref, ha_s.at[1], ha_r.at[1], along_y(i), q)

    wait(pall.at[0:15], pz_r.at[0])
    for i in range(8):
        piece = pall[2 * i:2 * i + 2].reshape(128, 256).astype(F32).T
        y[:, 128 * i:128 * (i + 1)] = piece
        yb[0, 0:256, 128 * i:128 * (i + 1)] = piece.astype(BF)

    wait(drho.at[0:3, :, c, 0], dxy_r.at[2])
    for i in range(1, 4):
        ref = drho.at[lax.rem(ty + i, NY), :, c, 0]
        send(ref, ref, df_s.at[2], df_r.at[2], t, sibling)
    wait(drho.at[0:3, :, c, 1], dxy_r.at[3])
    for i in range(1, 4):
        ref = drho.at[:, lax.rem(tx + i, NX), c, 1]
        send(ref, ref, df_s.at[3], df_r.at[3], t, sibling)
    wait(drho.at[0, :, other, 0], df_r.at[0])
    wait(drho.at[0, :, other, 1], df_r.at[1])
    wait(drho.at[0:3, :, other, 0], df_r.at[2])
    wait(drho.at[0:3, :, other, 1], df_r.at[3])

    lane = lax.broadcasted_iota(jnp.int32, (8, 128), 1)
    row = lax.broadcasted_iota(jnp.int32, (8, 128), 0)

    def unpack(i, carry):
        squares, diagonal = carry
        block = drho[lax.div(i, NX), lax.rem(i, NX)].reshape(64, 1024).astype(F32).reshape(8, 8, 1024)
        g[:, i] = block
        on = lane == 8 * i + row
        for zo in range(NZ):
            squares = squares + block[zo] * block[zo]
            diagonal = diagonal + jnp.where(on, block[zo][:, 128 * zo:128 * (zo + 1)], 0.0)
        return squares, diagonal

    squares, diagonal = lax.fori_loop(
        0, NT, unpack, (jnp.zeros((8, 1024), F32), jnp.zeros((8, 128), F32))
    )
    trace = jnp.sum(diagonal, axis=(0, 1), keepdims=True)
    damping = trace * (0.01 / B)
    norm = jnp.sum(squares, axis=(0, 1), keepdims=True) + damping * (2.0 * trace + B * damping)
    scale = 1.0 / jnp.sqrt(norm)

    def damp(i):
        on = lane == 8 * i + row
        for zo in range(NZ):
            at = g[zo, i, :, 128 * zo:128 * (zo + 1)]
            g[zo, i, :, 128 * zo:128 * (zo + 1)] = at + jnp.where(on, damping, 0.0)

    each(0, NT, damp)

    def operand(i):
        gb[0, pl.ds(pl.multiple_of(i * 128, 128), 128), :] = g[i].reshape(128, 1024).astype(BF)

    each(0, NZ, operand)

    wait(hta.at[0:4, 0, 0:3], ha_r.at[0])
    wait(hta.at[4:8, 0, 0:3], ha_r.at[1])
    for i in range(1, 4):
        ref = hta.at[0:4, ty]
        send(ref, ref, ha_s.at[2], ha_r.at[2], along_y(i), q)
        ref = hta.at[4:8, :, tx]
        send(ref, ref, ha_s.at[3], ha_r.at[3], along_x(i), q)

    for k in range(ITERS - 1):
        def square(i):
            rows = pl.ds(pl.multiple_of(i * 256, 256), 256)
            product = dot(gb[k, rows, :], gb[k])
            old = g[pl.ds(2 * i, 2)].reshape(256, 1024)
            if k == 0:
                new = (2.0 * scale) * old - (scale * scale) * product
            else:
                new = 2.0 * old - product
            if k < ITERS - 2:
                g[pl.ds(2 * i, 2)] = new.reshape(2, 16, 8, 1024)
            gb[k + 1, rows, :] = new.astype(BF)

        each(0, 4, square)

    for k in range(ITERS):
        def apply(i):
            columns = pl.ds(pl.multiple_of(i * 256, 256), 256)
            if k == 0:
                step = scale * dot(yb[0, 0:256], gb[0, :, columns])
            else:
                both = dot(yb[k % 2], gb[k, :, columns])
                step = both[0:256] + both[256:512]
            new = 2.0 * y[:, columns] - step
            if k == ITERS - 1:
                new = new * scale
            high = new.astype(BF)
            low = (new - high.astype(F32)).astype(BF)
            if k < ITERS - 1:
                y[:, columns] = new
                yb[(k + 1) % 2, 0:256, columns] = high
                yb[(k + 1) % 2, 256:512, columns] = low
            else:
                yx[c, 0:256, columns] = high
                yx[c, 256:512, columns] = low

        each(0, 4, apply)

    send(yx.at[c], yx.at[c], yx_s.at[0], yx_r.at[0], t, sibling)

    wait(hta.at[0:4, 0:3], ha_r.at[2])
    wait(hta.at[4:8, 0:3], ha_r.at[3])
    for zo in range(NZ):
        block = hta[zo].reshape(128, 512)
        high = block.astype(BF)
        hh[128 * zo:128 * (zo + 1), :] = high
        hl[128 * zo:128 * (zo + 1), :] = (block - high.astype(F32)).astype(BF)

    def finish(part):
        rows = pl.ds(pl.multiple_of(part * 256, 256), 256)
        both = dot(yx[part], hh[...])
        correction = both[0:256] + both[256:512] + dot(yx[part, 0:256], hl[...])
        kept = m[rows, :].astype(F32)
        out_ref[rows, :] = (kept * (w[rows, :].astype(F32) - correction)).astype(BF)

    finish(c)
    wait(yx.at[other], yx_r.at[0])
    finish(other)

    wait(pt.at[z, other, c], sib_s.at[0])
    wait(pt.at[z, c, c], sib_s.at[1])
    for d in range(2):
        for k in range(1, 5):
            for v in units(d, k):
                wait(pt.at[z, c, c], ring_s.at[hop(d, k, v)])
                wait(pt.at[z, c, c], fwd_s.at[hop(d, k, v)])
    for group in range(5):
        first, n = GROUPS[group]
        wait(hts.at[0:15, first:first + n], rs_s.at[group])
    wait(dsend.at[other], dsib_s.at[0])
    wait(drho.at[ty, tx, c, :, :, 0:896], dz_s.at[0])
    wait(pall.at[0:15], pz_s.at[0])
    wait(drho.at[0, 0:3, c, 0], dxy_s.at[0])
    wait(drho.at[0, 0:3, c, 1], dxy_s.at[1])
    wait(drho.at[0:3, :, c, 0], dxy_s.at[2])
    wait(drho.at[0:3, :, c, 1], dxy_s.at[3])
    wait(drho.at[0, :, c, 0], df_s.at[0])
    wait(drho.at[0, :, c, 1], df_s.at[1])
    wait(drho.at[0:3, :, c, 0], df_s.at[2])
    wait(drho.at[0:3, :, c, 1], df_s.at[3])
    wait(hta.at[0:4, 0, 0:3], ha_s.at[0])
    wait(hta.at[4:8, 0, 0:3], ha_s.at[1])
    wait(hta.at[0:4, 0:3], ha_s.at[2])
    wait(hta.at[4:8, 0:3], ha_s.at[3])
    wait(yx.at[c], yx_s.at[0])


def per_device(activations, weight, keep_mask):
    sems = (4, 2, 2, 14, 14, 14, 14, 5, 5, 1, 1, 1, 1, 4, 4, 4, 4, 1, 1, 4, 4, 1, 1)
    return pl.pallas_call(
        kernel,
        out_shape=jax.ShapeDtypeStruct(weight.shape, BF),
        in_specs=[pl.BlockSpec(memory_space=pl.ANY)] * 3,
        out_specs=pl.BlockSpec(memory_space=pltpu.VMEM),
        scratch_shapes=[
            pltpu.VMEM((2048, 512), BF),
            pltpu.VMEM((512, 512), BF),
            pltpu.VMEM((512, 512), jnp.int32),
            pltpu.VMEM((NZ, 2, 2, WIDTH, 1024), BF),
            pltpu.VMEM((NT, 8, 8, 512), F32),
            pltpu.VMEM((NT, 8, 8, 512), F32),
            pltpu.VMEM((NZ, 8, 512), F32),
            pltpu.VMEM((2, 32, 128), BF),
            pltpu.VMEM((32, 128), BF),
            pltpu.VMEM((2, 16, 128), BF),
            pltpu.VMEM((NY, NX, 2, 2, 16, 1024), BF),
            pltpu.VMEM((NZ, NT, 8, 1024), F32),
            pltpu.VMEM((ITERS, 1024, 1024), BF),
            pltpu.VMEM((NZ, NY, NX, 8, 512), F32),
            pltpu.VMEM((1024, 512), BF),
            pltpu.VMEM((1024, 512), BF),
            pltpu.VMEM((2, WIDTH, 256), BF),
            pltpu.VMEM((NQ, WIDTH, 256), BF),
            pltpu.VMEM((256, 1024), F32),
            pltpu.VMEM((2, 512, 1024), BF),
            pltpu.VMEM((2, 512, 1024), BF),
        ] + [pltpu.SemaphoreType.DMA((n,)) for n in sems],
        compiler_params=pltpu.CompilerParams(
            collective_id=0, has_side_effects=True, vmem_limit_bytes=56 << 20
        ),
    )(activations, weight, keep_mask)


def solution(mesh):
    return jax.shard_map(
        per_device,
        mesh=mesh,
        in_specs=(P("tok", "col"), P("tok", "col"), P("tok", "col")),
        out_specs=P("tok", "col"),
        check_vma=False,
    )
```

time: 285 us -> 87.9 us (0.31)
  waiting for transfers between devices: 223 us -> 0 us
  Pallas kernels: 0 us -> 85.9 us
  matrix products: 31.6 us -> 0 us
  between operations: 14.6 us -> 0.01 us
  other arithmetic: 9.21 us -> 0 us
  local copies, waits for them, and re-layouts: 6.38 us -> 1.87 us
    all_gather x3 -> x0, waiting for transfers between devices: 127 us -> none  [the longest x1 46.8 us: per_device(): lax.all_gather(activations[:, :panel_width], 'col', axis=1, tiled=True)]
    psum x1 -> x0, waiting for transfers between devices: 95.8 us -> none  [per_device(): hessian_panel = lax.psum(partial_panel, 'tok') / total_count]
    pallas_call x0 -> x1, Pallas kernels: none -> 85.9 us  [per_device(): pl.pallas_call(kernel, out_shape=jax.ShapeDtypeStruct(weight.shape, BF),...]
    dot_general x15 -> x0, matrix products: 31.6 us -> none  [mm(): return lax.dot_general(a, b, dims, preferred_element_type=jnp.float32)]
    reduce_sum x2 -> x0, other arithmetic: 6.8 us -> none  [the longest x1 3.88 us: per_device(): scale = lax.rsqrt(jnp.sum(damped * damped))]
  transfers between devices with their start and end apart: 4 -> 0, of which waited for: 4 -> 0; matrix products, arithmetic and copies ran while one was open for 2% -> 0% of each run, Pallas kernels for 0% -> 0%
where the time goes in v2:
time: 87.9 us; the launch traced here: 87.7 us
  Pallas kernels  85.9 us (98%)
  local copies, waits for them, and re-layouts  1.87 us (2%)
    pallas_call x1, Pallas kernels, per_device(): pl.pallas_call(kernel, out_shape=jax.ShapeDtypeStruct(weight.shape, BF),...  85.9 us
    unnamed x1, local copies, waits for them, and re-layouts  1.87 us

profile of v2, /device:TPU:1, one launch (start us, length us, event | category | flops | bytes accessed | tf_op | source)
XLA Modules:
  0.0 87.7 jit_solution(4688767846790189782)
XLA Ops:
  0.0 85.9 %shard_map.37 = bf16[512,512]{1,0:T(8,128)(2,1)} custom-call(bf16[2048,512]{1,0:T(8,128)(2,1)} %a_hbm.1, bf16[512,512]{1,0:T(8,128)(2,1)} %w_hbm.1, s32[512,512]{1,0:T(8,128)} %m_hbm.1), custom_call_target="tpu_custom_call" | custom-call | tf_op jit(solution)/shard_map/pallas_call | solution.py:379
  85.9 1.9 %copy.5 = bf16[512,512]{1,0:T(8,128)(2,1)} copy(bf16[512,512]{1,0:T(8,128)(2,1)} %shard_map.37) | data formatting | bytes 1048576

commit v3 on v2

v3 whole, which is shorter than its diff:
```python
import functools

import jax
import jax.numpy as jnp
from jax import lax
from jax.experimental import pallas as pl
from jax.experimental.pallas import tpu as pltpu
from jax.sharding import PartitionSpec as P

B = 1024
ITERS = 4
NZ, NY, NX, NT, NQ = 8, 4, 4, 16, 16
WIDTH = 64
OFFSETS = (0, -1, 1, -2, 2, -3, 3, 4)
GROUPS = ((0, 1), (7, 1), (5, 2), (3, 2), (1, 2))
EARLY = (slice(0, 2), slice(2, 4))
PAIRS = ((1, 2), (3, 4), (5, 6), (0, 7))
BATCHES = (slice(5, 8), slice(0, 5))
BF, F32 = jnp.bfloat16, jnp.float32


def dot(a, b):
    return jnp.dot(a, b, preferred_element_type=F32)


def kernel(
    a_hbm, w_hbm, m_hbm, out_ref,
    a, w, m, pt, hts, ks, kr, r1, p1, r2, red, dn, dsend, drecv, dzs, drho, g, gb, hta, hh, hl, pts, pall, y, yb, yx,
    load_sem, sib_s, sib_r, ring_s, ring_r, fwd_s, fwd_r, rs_s, rs_r, r1_s, r1_r, r2_s, r2_r, dsib_s, dsib_r, dz_s, dz_r,
    dxy_s, dxy_r, df_s, df_r, pz_s, pz_r, ha_s, ha_r, yx_s, yx_r,
):
    t, q = lax.axis_index("tok"), lax.axis_index("col")
    ty, tx = lax.div(t, NX), lax.rem(t, NX)
    z, c = lax.div(q, 2), lax.rem(q, 2)
    other = 1 - c
    sibling = 2 * z + other
    inverse_count = 1.0 / (a.shape[0] * NT)

    def send(src, dst, send_sem, recv_sem, tok, col):
        pltpu.make_async_remote_copy(
            src_ref=src, dst_ref=dst, send_sem=send_sem, recv_sem=recv_sem,
            device_id=(tok, col), device_id_type=pl.DeviceIdType.MESH,
        ).start()

    def wait(ref, sem):
        pltpu.make_async_copy(ref, ref, sem).wait()

    def each(first, last, body):
        def step(i, carry):
            body(i)
            return carry
        lax.fori_loop(first, last, step, 0)

    loads = [
        pltpu.make_async_copy(a_hbm.at[:, 0:128], a.at[:, 0:128], load_sem.at[0]),
        pltpu.make_async_copy(a_hbm.at[:, 128:512], a.at[:, 128:512], load_sem.at[1]),
        pltpu.make_async_copy(w_hbm, w, load_sem.at[2]),
        pltpu.make_async_copy(m_hbm, m, load_sem.at[3]),
    ]
    for load in loads:
        load.start()

    barrier = pltpu.get_barrier_semaphore()

    def greet(i):
        pl.semaphore_signal(
            barrier, inc=1, device_id=(lax.rem(t + i, NT), q), device_id_type=pl.DeviceIdType.MESH
        )
        pl.semaphore_signal(
            barrier, inc=1, device_id=(t, lax.rem(q + i, NQ)), device_id_type=pl.DeviceIdType.MESH
        )

    each(1, 16, greet)

    loads[0].wait()
    for half in range(2):
        for part in range(2):
            rows = half * 1024 + part * 512
            piece = a[rows:rows + 512, 0:128].astype(F32).T
            pt[z, half, c, :, part * 512:(part + 1) * 512] = piece[0:WIDTH].astype(BF)
    pl.semaphore_wait(barrier, 30)

    following = lax.rem(z + NZ + 1 - 2 * c, NZ)

    def origin(k, core):
        return lax.rem(z + NZ + (2 * core - 1) * k, NZ)

    def ring(k, v):
        u = c if v < 2 else other
        ref = pt.at[origin(k - 1, c), c, u, 32 * (v % 2):32 * (v % 2) + 32]
        at = 4 * (k - 1) + v
        send(ref, ref, ring_s.at[at], ring_r.at[at], t, 2 * following + c)

    send(pt.at[z, other, c], pt.at[z, other, c], sib_s.at[0], sib_r.at[0], t, sibling)
    ring(1, 0)
    ring(1, 1)
    send(pt.at[z, c, c], pt.at[z, c, c], sib_s.at[1], sib_r.at[1], t, sibling)
    wait(pt.at[z, c, other], sib_r.at[0])
    ring(1, 2)
    ring(1, 3)

    loads[2].wait()
    loads[3].wait()
    pruned = jnp.where(m[:, 0:128] == 0, w[:, 0:128].astype(F32), 0.0).T
    pts[0] = pruned[0:WIDTH, 0:256].astype(BF)
    pts[1] = pruned[0:WIDTH, 256:512].astype(BF)
    pall[q] = pts[c]

    loads[1].wait()
    wait(pt.at[z, other, other], sib_r.at[1])

    def along_x(i):
        return NX * ty + lax.rem(tx + i, NX)

    def along_y(i):
        return NX * lax.rem(ty + i, NY) + tx

    def chunk_at(slot):
        return lax.rem(z + OFFSETS[slot] + NZ, NZ)

    def product(chunk, half):
        rows = pt[chunk, half].reshape(128, 1024)
        return dot(rows, a[1024 * half:1024 * (half + 1), :])

    def pass_on(k):
        for v in range(4):
            u = c if v < 2 else other
            wait(
                pt.at[origin(k, c), c, u, 32 * (v % 2):32 * (v % 2) + 32], ring_r.at[4 * (k - 1) + v]
            )
            if k < 7:
                ring(k + 1, v)
            if v % 2 == 1:
                ref = pt.at[origin(k, c), c, u]
                at = 2 * (k - 1) + v // 2
                send(ref, ref, fwd_s.at[at], fwd_r.at[at], t, sibling)

    def side_by_side(left, right):
        lanes = lax.broadcasted_iota(jnp.int32, (128, 128), 1)
        packed = jnp.where(lanes < WIDTH, left[:, 0:128], pltpu.roll(right[:, 0:128], WIDTH, 1))
        return packed.reshape(NY, NX, 8, 128)

    def multiply(k):
        wait(pt.at[origin(k, other), other, other], fwd_r.at[2 * (k - 1)])
        wait(pt.at[origin(k, other), other, c], fwd_r.at[2 * (k - 1) + 1])
        below, above = product(origin(k, 0), 0), product(origin(k, 1), 1)
        if k < 4:
            hts[:, :, 2 * k - 1] = below.reshape(NY, NX, 8, 512)
            hts[:, :, 2 * k] = above.reshape(NY, NX, 8, 512)
            ks[:, :, k - 1] = side_by_side(below, above)
        elif k == 4:
            both = below + above
            hts[:, :, 7] = both.reshape(NY, NX, 8, 512)
            own = hts[:, :, 0].reshape(128, 512)
            ks[:, :, 3] = 0.5 * side_by_side(own, both)
        else:
            d = 8 - k
            hts[:, :, 2 * d] = hts[:, :, 2 * d] + below.reshape(NY, NX, 8, 512)
            hts[:, :, 2 * d - 1] = hts[:, :, 2 * d - 1] + above.reshape(NY, NX, 8, 512)

    def share_early(part):
        slots = EARLY[part]
        kr[t, slots] = ks[ty, tx, slots]

        def to_peer(i):
            to = lax.rem(t + i, NT)
            send(
                ks.at[lax.div(to, NX), lax.rem(to, NX), slots], kr.at[t, slots],
                rs_s.at[part], rs_r.at[part], to, q,
            )

        each(1, 16, to_peer)

    def reduce_early(part):
        slots = EARLY[part]
        wait(kr.at[0:15, slots], rs_r.at[part])
        total = kr[0, slots]
        for source in range(1, NT):
            total = total + kr[source, slots]
        total = total * inverse_count
        for i in range(2):
            left, right = PAIRS[slots.start + i]
            dn[chunk_at(left)] = total[i]
            dn[chunk_at(right)] = pltpu.roll(total[i], WIDTH, 1)

    def first_phase(group):
        first, n = GROUPS[group]
        slots = slice(first, first + n)
        r1[0, tx, :, slots] = hts[:, tx, slots, :, 0:256]
        r1[1, ty, :, slots] = hts[ty, :, slots, :, 256:512]
        for i in range(1, 4):
            send(
                hts.at[:, lax.rem(tx + i, NX), slots, :, 0:256], r1.at[0, tx, :, slots],
                r1_s.at[2 * group], r1_r.at[2 * group], along_x(i), q,
            )
            send(
                hts.at[lax.rem(ty + i, NY), :, slots, :, 256:512], r1.at[1, ty, :, slots],
                r1_s.at[2 * group + 1], r1_r.at[2 * group + 1], along_y(i), q,
            )

    def second_phase(group):
        first, n = GROUPS[group]
        slots = slice(first, first + n)
        for part in range(2):
            wait(r1.at[part, 0:3, :, slots], r1_r.at[2 * group + part])
            p1[part, :, slots] = (
                (r1[part, 0, :, slots] + r1[part, 1, :, slots])
                + (r1[part, 2, :, slots] + r1[part, 3, :, slots])
            )
            me, size = (ty, NY) if part == 0 else (tx, NX)
            r2[part, me, slots] = p1[part, me, slots]
            for i in range(1, 4):
                send(
                    p1.at[part, lax.rem(me + i, size), slots], r2.at[part, me, slots],
                    r2_s.at[2 * group + part], r2_r.at[2 * group + part],
                    along_y(i) if part == 0 else along_x(i), q,
                )

    def reduce_group(group):
        first, n = GROUPS[group]
        slots = slice(first, first + n)
        for part in range(2):
            wait(r2.at[part, 0:3, slots], r2_r.at[2 * group + part])
            total = (r2[part, 0, slots] + r2[part, 1, slots]) + (r2[part, 2, slots] + r2[part, 3, slots])
            red[slots, :, 256 * part:256 * (part + 1)] = total * inverse_count

    def gather_first(batch):
        slots = BATCHES[batch]
        hta[slots, ty, tx] = red[slots]
        for i in range(1, 4):
            ref = hta.at[slots, ty, tx, :, 0:256]
            send(ref, ref, ha_s.at[4 * batch], ha_r.at[4 * batch], along_x(i), q)
            ref = hta.at[slots, ty, tx, :, 256:512]
            send(ref, ref, ha_s.at[4 * batch + 1], ha_r.at[4 * batch + 1], along_y(i), q)

    def gather_second(batch):
        slots = BATCHES[batch]
        wait(hta.at[slots, 0, 0:3, :, 0:256], ha_r.at[4 * batch])
        wait(hta.at[slots, 0, 0:3, :, 256:512], ha_r.at[4 * batch + 1])
        for i in range(1, 4):
            ref = hta.at[slots, ty, :, :, 0:256]
            send(ref, ref, ha_s.at[4 * batch + 2], ha_r.at[4 * batch + 2], along_y(i), q)
            ref = hta.at[slots, :, tx, :, 256:512]
            send(ref, ref, ha_s.at[4 * batch + 3], ha_r.at[4 * batch + 3], along_x(i), q)

    def gather_end(batch):
        slots = BATCHES[batch]
        wait(hta.at[slots, 0:3, :, :, 0:256], ha_r.at[4 * batch + 2])
        wait(hta.at[slots, 0:3, :, :, 256:512], ha_r.at[4 * batch + 3])
        for slot in range(slots.start, slots.stop):
            rows = pl.ds(pl.multiple_of(128 * chunk_at(slot), 128), 128)
            block = hta[slot].reshape(128, 512)
            high = block.astype(BF)
            hh[rows, :] = high
            hl[rows, :] = (block - high.astype(F32)).astype(BF)

    own = product(z, 0) + product(z, 1)
    hts[:, :, 0] = own.reshape(NY, NX, 8, 512)
    first_phase(0)
    pass_on(1)
    multiply(1)
    pass_on(2)
    multiply(2)
    share_early(0)
    second_phase(0)
    pass_on(3)
    multiply(3)
    reduce_group(0)
    pass_on(4)
    multiply(4)
    share_early(1)
    first_phase(1)
    reduce_early(0)
    pass_on(5)
    multiply(5)
    first_phase(2)
    reduce_early(1)

    lanes = lax.broadcasted_iota(jnp.int32, (64, 128), 1)
    own = dn[...].reshape(64, 128)
    own = jnp.where(c == 0, own, pltpu.roll(own, 64, 1))
    own = jnp.where(lax.div(lanes, 64) == c, own, 0.0)
    dsend[0] = own[0:32].astype(BF)
    dsend[1] = own[32:64].astype(BF)
    send(dsend.at[other], drecv, dsib_s.at[0], dsib_r.at[0], t, sibling)
    pass_on(6)
    wait(drecv, dsib_r.at[0])
    here = (dsend[c].astype(F32) + drecv[...].astype(F32)).astype(BF).reshape(2, 16, 128)
    dzs[...] = here
    my_lanes = pl.ds(pl.multiple_of(z * 128, 128), 128)
    drho[ty, tx, c, :, :, my_lanes] = here

    def along_z(i):
        send(
            dzs, drho.at[ty, tx, c, :, :, my_lanes], dz_s.at[0], dz_r.at[0],
            t, 2 * lax.rem(z + i, NZ) + c,
        )

    each(1, NZ, along_z)

    multiply(6)
    first_phase(3)
    second_phase(1)
    pass_on(7)
    second_phase(2)
    multiply(7)
    first_phase(4)

    wait(drho.at[ty, tx, c, :, :, 0:896], dz_r.at[0])

    for i in range(1, 4):
        ref = drho.at[ty, tx, c, 0]
        send(ref, ref, dxy_s.at[0], dxy_r.at[0], along_x(i), q)
        ref = drho.at[ty, tx, c, 1]
        send(ref, ref, dxy_s.at[1], dxy_r.at[1], along_y(i), q)
    reduce_group(1)
    reduce_group(2)
    gather_first(0)
    second_phase(3)
    wait(drho.at[0, 0:3, c, 0], dxy_r.at[0])
    for i in range(1, 4):
        ref = drho.at[ty, :, c, 0]
        send(ref, ref, dxy_s.at[2], dxy_r.at[2], along_y(i), q)
    wait(drho.at[0, 0:3, c, 1], dxy_r.at[1])
    for i in range(1, 4):
        ref = drho.at[:, tx, c, 1]
        send(ref, ref, dxy_s.at[3], dxy_r.at[3], along_x(i), q)
    ref = drho.at[ty, :, c, 0]
    send(ref, ref, df_s.at[0], df_r.at[0], t, sibling)
    ref = drho.at[:, tx, c, 1]
    send(ref, ref, df_s.at[1], df_r.at[1], t, sibling)

    def share_pruned(i):
        to = lax.rem(q + i, NQ)
        send(pts.at[lax.rem(to, 2)], pall.at[q], pz_s.at[0], pz_r.at[0], t, to)

    each(1, NQ, share_pruned)

    second_phase(4)
    reduce_group(3)
    gather_second(0)
    reduce_group(4)
    gather_first(1)
    wait(drho.at[0:3, :, c, 0], dxy_r.at[2])
    for i in range(1, 4):
        ref = drho.at[lax.rem(ty + i, NY), :, c, 0]
        send(ref, ref, df_s.at[2], df_r.at[2], t, sibling)
    wait(drho.at[0:3, :, c, 1], dxy_r.at[3])
    for i in range(1, 4):
        ref = drho.at[:, lax.rem(tx + i, NX), c, 1]
        send(ref, ref, df_s.at[3], df_r.at[3], t, sibling)
    gather_second(1)
    wait(drho.at[0, :, other, 0], df_r.at[0])
    wait(drho.at[0, :, other, 1], df_r.at[1])
    wait(drho.at[0:3, :, other, 0], df_r.at[2])
    wait(drho.at[0:3, :, other, 1], df_r.at[3])

    lane = lax.broadcasted_iota(jnp.int32, (8, 128), 1)
    row = lax.broadcasted_iota(jnp.int32, (8, 128), 0)
    diagonal = jnp.zeros((8, 128), F32)
    for i in range(NT):
        block = drho[i // NX, i % NX].reshape(64, 1024).astype(F32).reshape(8, 8, 1024)
        g[:, i] = block
        for zo in range(NZ):
            diagonal = diagonal + jnp.where(
                lane == 8 * i + row, block[zo][:, 128 * zo:128 * (zo + 1)], 0.0
            )
    trace = 2.0 * jnp.sum(diagonal, axis=(0, 1), keepdims=True)
    damping = trace * (0.01 / B)
    wide_row = lax.broadcasted_iota(jnp.int32, (256, 256), 0)
    wide_lane = lax.broadcasted_iota(jnp.int32, (256, 256), 1)
    squares = jnp.zeros((1, 256), F32)
    for i in range(4):
        for j in range(i, 4):
            upper = g[2 * i:2 * i + 2, :, :, 256 * j:256 * (j + 1)].reshape(256, 256)
            lower = g[2 * j:2 * j + 2, :, :, 256 * i:256 * (i + 1)].reshape(256, 256)
            block = upper + lower.T
            total = jnp.sum(block * block, axis=0, keepdims=True)
            squares = squares + (total if i == j else 2.0 * total)
            if i == j:
                block = block + jnp.where(wide_row == wide_lane, damping, 0.0)
            g[2 * i:2 * i + 2, :, :, 256 * j:256 * (j + 1)] = block.reshape(2, 16, 8, 256)
            gb[0, 256 * i:256 * (i + 1), 256 * j:256 * (j + 1)] = block.astype(BF)
            if i != j:
                gb[0, 256 * j:256 * (j + 1), 256 * i:256 * (i + 1)] = block.T.astype(BF)
    norm = jnp.sum(squares, axis=(0, 1), keepdims=True) + damping * (2.0 * trace + B * damping)
    scale = 1.0 / jnp.sqrt(norm)

    for k in range(ITERS - 1):
        for i in range(4):
            n = 1024 - 256 * i
            product = dot(gb[k, 256 * i:256 * (i + 1), :], gb[k, :, 256 * i:1024])
            old = g[2 * i:2 * i + 2, :, :, 256 * i:1024].reshape(256, n)
            if k == 0:
                new = (2.0 * scale) * old - (scale * scale) * product
            else:
                new = 2.0 * old - product
            if k < ITERS - 2:
                g[2 * i:2 * i + 2, :, :, 256 * i:1024] = new.reshape(2, 16, 8, n)
            gb[k + 1, 256 * i:256 * (i + 1), 256 * i:1024] = new.astype(BF)
            for j in range(i + 1, 4):
                mirrored = new[:, 256 * (j - i):256 * (j - i + 1)].T
                gb[k + 1, 256 * j:256 * (j + 1), 256 * i:256 * (i + 1)] = mirrored.astype(BF)

    wait(pall.at[0:15], pz_r.at[0])
    for i in range(8):
        piece = pall[2 * i:2 * i + 2].reshape(128, 256).astype(F32).T
        y[:, 128 * i:128 * (i + 1)] = piece
        yb[0, 0:256, 128 * i:128 * (i + 1)] = piece.astype(BF)

    for k in range(ITERS):
        for i in range(4):
            columns = slice(256 * i, 256 * (i + 1))
            if k == 0:
                step = scale * dot(yb[0, 0:256], gb[0, :, columns])
            else:
                both = dot(yb[k % 2], gb[k, :, columns])
                step = both[0:256] + both[256:512]
            new = 2.0 * y[:, columns] - step
            if k == ITERS - 1:
                new = new * scale
            high = new.astype(BF)
            low = (new - high.astype(F32)).astype(BF)
            if k < ITERS - 1:
                y[:, columns] = new
                yb[(k + 1) % 2, 0:256, columns] = high
                yb[(k + 1) % 2, 256:512, columns] = low
            else:
                yx[c, 0:256, columns] = high
                yx[c, 256:512, columns] = low

    send(yx.at[c], yx.at[c], yx_s.at[0], yx_r.at[0], t, sibling)

    gather_end(0)
    gather_end(1)

    def finish(part):
        rows = pl.ds(pl.multiple_of(part * 256, 256), 256)
        both = dot(yx[part], hh[...])
        correction = both[0:256] + both[256:512] + dot(yx[part, 0:256], hl[...])
        kept = m[rows, :].astype(F32)
        out_ref[rows, :] = (kept * (w[rows, :].astype(F32) - correction)).astype(BF)

    finish(c)
    wait(yx.at[other], yx_r.at[0])
    finish(other)

    wait(pt.at[z, other, c], sib_s.at[0])
    wait(pt.at[z, c, c], sib_s.at[1])
    for at in range(28):
        wait(pt.at[z, c, c, 0:32], ring_s.at[at])
    for at in range(14):
        wait(pt.at[z, c, c], fwd_s.at[at])
    for group in range(5):
        first, n = GROUPS[group]
        for part in range(2):
            wait(r1.at[part, 0:3, :, first:first + n], r1_s.at[2 * group + part])
            wait(r2.at[part, 0:3, first:first + n], r2_s.at[2 * group + part])
    for part in range(2):
        wait(kr.at[0:15, EARLY[part]], rs_s.at[part])
    wait(dsend.at[other], dsib_s.at[0])
    wait(drho.at[ty, tx, c, :, :, 0:896], dz_s.at[0])
    wait(pall.at[0:15], pz_s.at[0])
    wait(drho.at[0, 0:3, c, 0], dxy_s.at[0])
    wait(drho.at[0, 0:3, c, 1], dxy_s.at[1])
    wait(drho.at[0:3, :, c, 0], dxy_s.at[2])
    wait(drho.at[0:3, :, c, 1], dxy_s.at[3])
    wait(drho.at[0, :, c, 0], df_s.at[0])
    wait(drho.at[0, :, c, 1], df_s.at[1])
    wait(drho.at[0:3, :, c, 0], df_s.at[2])
    wait(drho.at[0:3, :, c, 1], df_s.at[3])
    for batch in range(2):
        slots = BATCHES[batch]
        wait(hta.at[slots, 0, 0:3, :, 0:256], ha_s.at[4 * batch])
        wait(hta.at[slots, 0, 0:3, :, 256:512], ha_s.at[4 * batch + 1])
        wait(hta.at[slots, 0:3, :, :, 0:256], ha_s.at[4 * batch + 2])
        wait(hta.at[slots, 0:3, :, :, 256:512], ha_s.at[4 * batch + 3])
    wait(yx.at[c], yx_s.at[0])


def per_device(activations, weight, keep_mask):
    sems = (4, 2, 2, 28, 28, 14, 14, 2, 2, 10, 10, 10, 10, 1, 1, 1, 1, 4, 4, 4, 4, 1, 1, 8, 8, 1, 1)
    return pl.pallas_call(
        kernel,
        out_shape=jax.ShapeDtypeStruct(weight.shape, BF),
        in_specs=[pl.BlockSpec(memory_space=pl.ANY)] * 3,
        out_specs=pl.BlockSpec(memory_space=pltpu.VMEM),
        scratch_shapes=[
            pltpu.VMEM((2048, 512), BF),
            pltpu.VMEM((512, 512), BF),
            pltpu.VMEM((512, 512), jnp.int32),
            pltpu.VMEM((NZ, 2, 2, WIDTH, 1024), BF),
            pltpu.VMEM((NY, NX, 8, 8, 512), F32),
            pltpu.VMEM((NY, NX, 4, 8, 128), F32),
            pltpu.VMEM((NT, 4, 8, 128), F32),
            pltpu.VMEM((2, 4, 4, 8, 8, 256), F32),
            pltpu.VMEM((2, 4, 8, 8, 256), F32),
            pltpu.VMEM((2, 4, 8, 8, 256), F32),
            pltpu.VMEM((8, 8, 512), F32),
            pltpu.VMEM((NZ, 8, 128), F32),
            pltpu.VMEM((2, 32, 128), BF),
            pltpu.VMEM((32, 128), BF),
            pltpu.VMEM((2, 16, 128), BF),
            pltpu.VMEM((NY, NX, 2, 2, 16, 1024), BF),
            pltpu.VMEM((NZ, NT, 8, 1024), F32),
            pltpu.VMEM((ITERS, 1024, 1024), BF),
            pltpu.VMEM((NZ, NY, NX, 8, 512), F32),
            pltpu.VMEM((1024, 512), BF),
            pltpu.VMEM((1024, 512), BF),
            pltpu.VMEM((2, WIDTH, 256), BF),
            pltpu.VMEM((NQ, WIDTH, 256), BF),
            pltpu.VMEM((256, 1024), F32),
            pltpu.VMEM((2, 512, 1024), BF),
            pltpu.VMEM((2, 512, 1024), BF),
        ] + [pltpu.SemaphoreType.DMA((n,)) for n in sems],
        compiler_params=pltpu.CompilerParams(
            collective_id=0, has_side_effects=True, vmem_limit_bytes=56 << 20
        ),
    )(activations, weight, keep_mask)


def solution(mesh):
    return jax.shard_map(
        per_device,
        mesh=mesh,
        in_specs=(P("tok", "col"), P("tok", "col"), P("tok", "col")),
        out_specs=P("tok", "col"),
        check_vma=False,
    )
```

time: 87.9 us -> 81.2 us (0.924)
  Pallas kernels: 85.9 us -> 79.2 us
    pallas_call x1, Pallas kernels: 85.9 us -> 79.2 us  [per_device(): pl.pallas_call(kernel, out_shape=jax.ShapeDtypeStruct(weight.shape, BF),...]
where the time goes in v3:
time: 81.2 us; the launch traced here: 81.1 us
  Pallas kernels  79.2 us (98%)
  local copies, waits for them, and re-layouts  1.87 us (2%)
    pallas_call x1, Pallas kernels, per_device(): pl.pallas_call(kernel, out_shape=jax.ShapeDtypeStruct(weight.shape, BF),...  79.2 us
    unnamed x1, local copies, waits for them, and re-layouts  1.87 us

profile of v3, /device:TPU:1, one launch (start us, length us, event | category | flops | bytes accessed | tf_op | source)
XLA Modules:
  0.0 81.1 jit_solution(12366595136243772061)
XLA Ops:
  0.0 79.2 %shard_map.37 = bf16[512,512]{1,0:T(8,128)(2,1)} custom-call(bf16[2048,512]{1,0:T(8,128)(2,1)} %a_hbm.1, bf16[512,512]{1,0:T(8,128)(2,1)} %w_hbm.1, s32[512,512]{1,0:T(8,128)} %m_hbm.1), custom_call_target="tpu_custom_call" | custom-call | tf_op jit(solution)/shard_map/pallas_call | solution.py:483
  79.2 1.9 %copy.5 = bf16[512,512]{1,0:T(8,128)(2,1)} copy(bf16[512,512]{1,0:T(8,128)(2,1)} %shard_map.37) | data formatting | bytes 1048576

commit v4 on v3

--- a/solution.py
+++ b/solution.py
@@ -86,18 +86,18 @@
         return lax.rem(z + NZ + (2 * core - 1) * k, NZ)
 
     def ring(k, v):
-        u = c if v < 2 else other
-        ref = pt.at[origin(k - 1, c), c, u, 32 * (v % 2):32 * (v % 2) + 32]
-        at = 4 * (k - 1) + v
+        u = c if v < 4 else other
+        ref = pt.at[origin(k - 1, c), c, u, 16 * (v % 4):16 * (v % 4) + 16]
+        at = 8 * (k - 1) + v
         send(ref, ref, ring_s.at[at], ring_r.at[at], t, 2 * following + c)
 
     send(pt.at[z, other, c], pt.at[z, other, c], sib_s.at[0], sib_r.at[0], t, sibling)
-    ring(1, 0)
-    ring(1, 1)
+    for v in range(4):
+        ring(1, v)
     send(pt.at[z, c, c], pt.at[z, c, c], sib_s.at[1], sib_r.at[1], t, sibling)
     wait(pt.at[z, c, other], sib_r.at[0])
-    ring(1, 2)
-    ring(1, 3)
+    for v in range(4, 8):
+        ring(1, v)
 
     loads[2].wait()
     loads[3].wait()
@@ -123,16 +123,16 @@
         return dot(rows, a[1024 * half:1024 * (half + 1), :])
 
     def pass_on(k):
-        for v in range(4):
-            u = c if v < 2 else other
+        for v in range(8):
+            u = c if v < 4 else other
             wait(
-                pt.at[origin(k, c), c, u, 32 * (v % 2):32 * (v % 2) + 32], ring_r.at[4 * (k - 1) + v]
+                pt.at[origin(k, c), c, u, 16 * (v % 4):16 * (v % 4) + 16], ring_r.at[8 * (k - 1) + v]
             )
             if k < 7:
                 ring(k + 1, v)
-            if v % 2 == 1:
+            if v % 4 == 3:
                 ref = pt.at[origin(k, c), c, u]
-                at = 2 * (k - 1) + v // 2
+                at = 2 * (k - 1) + v // 4
                 send(ref, ref, fwd_s.at[at], fwd_r.at[at], t, sibling)
 
     def side_by_side(left, right):
@@ -317,6 +317,7 @@
     reduce_group(2)
     gather_first(0)
     second_phase(3)
+    second_phase(4)
     wait(drho.at[0, 0:3, c, 0], dxy_r.at[0])
     for i in range(1, 4):
         ref = drho.at[ty, :, c, 0]
@@ -336,9 +337,7 @@
 
     each(1, NQ, share_pruned)
 
-    second_phase(4)
     reduce_group(3)
-    gather_second(0)
     reduce_group(4)
     gather_first(1)
     wait(drho.at[0:3, :, c, 0], dxy_r.at[2])
@@ -349,6 +348,7 @@
     for i in range(1, 4):
         ref = drho.at[:, lax.rem(tx + i, NX), c, 1]
         send(ref, ref, df_s.at[3], df_r.at[3], t, sibling)
+    gather_second(0)
     gather_second(1)
     wait(drho.at[0, :, other, 0], df_r.at[0])
     wait(drho.at[0, :, other, 1], df_r.at[1])
@@ -447,8 +447,8 @@
 
     wait(pt.at[z, other, c], sib_s.at[0])
     wait(pt.at[z, c, c], sib_s.at[1])
-    for at in range(28):
-        wait(pt.at[z, c, c, 0:32], ring_s.at[at])
+    for at in range(56):
+        wait(pt.at[z, c, c, 0:16], ring_s.at[at])
     for at in range(14):
         wait(pt.at[z, c, c], fwd_s.at[at])
     for group in range(5):
@@ -479,7 +479,7 @@
 
 
 def per_device(activations, weight, keep_mask):
-    sems = (4, 2, 2, 28, 28, 14, 14, 2, 2, 10, 10, 10, 10, 1, 1, 1, 1, 4, 4, 4, 4, 1, 1, 8, 8, 1, 1)
+    sems = (4, 2, 2, 56, 56, 14, 14, 2, 2, 10, 10, 10, 10, 1, 1, 1, 1, 4, 4, 4, 4, 1, 1, 8, 8, 1, 1)
     return pl.pallas_call(
         kernel,
         out_shape=jax.ShapeDtypeStruct(weight.shape, BF),

time: 81.2 us -> 78.2 us (0.963)
  Pallas kernels: 79.2 us -> 76.2 us
    pallas_call x1, Pallas kernels: 79.2 us -> 76.2 us  [per_device(): pl.pallas_call(kernel, out_shape=jax.ShapeDtypeStruct(weight.shape, BF),...]
where the time goes in v4:
time: 78.2 us; the launch traced here: 78 us
  Pallas kernels  76.2 us (97%)
  local copies, waits for them, and re-layouts  1.87 us (2%)
    pallas_call x1, Pallas kernels, per_device(): pl.pallas_call(kernel, out_shape=jax.ShapeDtypeStruct(weight.shape, BF),...  76.2 us
    unnamed x1, local copies, waits for them, and re-layouts  1.87 us

profile of v4, /device:TPU:1, one launch (start us, length us, event | category | flops | bytes accessed | tf_op | source)
XLA Modules:
  0.0 78.0 jit_solution(10367781079685635126)
XLA Ops:
  0.0 76.2 %shard_map.37 = bf16[512,512]{1,0:T(8,128)(2,1)} custom-call(bf16[2048,512]{1,0:T(8,128)(2,1)} %a_hbm.1, bf16[512,512]{1,0:T(8,128)(2,1)} %w_hbm.1, s32[512,512]{1,0:T(8,128)} %m_hbm.1), custom_call_target="tpu_custom_call" | custom-call | tf_op jit(solution)/shard_map/pallas_call | solution.py:483
  76.2 1.9 %copy.5 = bf16[512,512]{1,0:T(8,128)(2,1)} copy(bf16[512,512]{1,0:T(8,128)(2,1)} %shard_map.37) | data formatting | bytes 1048576

commit v5 on v4

--- a/solution.py
+++ b/solution.py
@@ -409,6 +409,8 @@
         yb[0, 0:256, 128 * i:128 * (i + 1)] = piece.astype(BF)
 
     for k in range(ITERS):
+        if k == ITERS - 1:
+            gather_end(0)
         for i in range(4):
             columns = slice(256 * i, 256 * (i + 1))
             if k == 0:
@@ -431,7 +433,6 @@
 
     send(yx.at[c], yx.at[c], yx_s.at[0], yx_r.at[0], t, sibling)
 
-    gather_end(0)
     gather_end(1)
 
     def finish(part):

time: 78.2 us -> 78.2 us (level)
  no operation moved by 1% of the time
where the time goes in v5:
time: 78.2 us; the launch traced here: 78 us
  Pallas kernels  76.2 us (97%)
  local copies, waits for them, and re-layouts  1.87 us (2%)
    pallas_call x1, Pallas kernels, per_device(): pl.pallas_call(kernel, out_shape=jax.ShapeDtypeStruct(weight.shape, BF),...  76.2 us
    unnamed x1, local copies, waits for them, and re-layouts  1.87 us

profile of v5, /device:TPU:1, one launch (start us, length us, event | category | flops | bytes accessed | tf_op | source)
XLA Modules:
  0.0 78.0 jit_solution(12176347429892037983)
XLA Ops:
  0.0 76.2 %shard_map.37 = bf16[512,512]{1,0:T(8,128)(2,1)} custom-call(bf16[2048,512]{1,0:T(8,128)(2,1)} %a_hbm.1, bf16[512,512]{1,0:T(8,128)(2,1)} %w_hbm.1, s32[512,512]{1,0:T(8,128)} %m_hbm.1), custom_call_target="tpu_custom_call" | custom-call | tf_op jit(solution)/shard_map/pallas_call | solution.py:484
  76.2 1.9 %copy.5 = bf16[512,512]{1,0:T(8,128)(2,1)} copy(bf16[512,512]{1,0:T(8,128)(2,1)} %shard_map.37) | data formatting | bytes 1048576
